TPU v7x, 512 devices: a whole 4x4x16 slice. The times are simulated.
512 devices in a mesh: tile: 32 (over y, x, core), depth: 16 (over z).
Axes of the slice: x: 4, y: 4, z: 16, core: 2. Of those that a mesh axis runs over, the one named last changes fastest.
Arguments:
- features: bfloat16 [16, 8192, 128], P('depth', 'tile'), may hold values from -4 to 4
- logits: float32 [16, 8192], P('depth', 'tile'), may hold values from -2.75 to 5.5
- geometry: float32 [2, 16, 5, 8192], P(None, 'depth', None, 'tile'), may hold values from -0.6 to 32, as said below
- dest_slot: int32 [2, 16, 8192], P(None, 'depth', 'tile'), may hold values from -1 to 8191, as said below
- target: bfloat16 [2, 64, 128, 1024], P(None, 'tile'), may hold values from -3 to 3
Outputs:
- images: bfloat16 [2, 64, 128, 1024], P(None, 'tile', None, 'depth')
- new_features: bfloat16 [16, 8192, 128], P('depth', 'tile')
- new_logits: float32 [16, 8192], P('depth', 'tile')
- shape_grads: float32 [2, 16, 5, 8192], P(None, 'depth', None, 'tile')
Inputs may be any that keep to these rules, and one draw needn't show every extreme that they name: `dest_slot`: for each view and layer no two splats share a slot; -1 marks a splat outside the view; a splat's place within its tile is its front-to-back order. At most 8 splats of one layer held by one index of tile go to the tiles of one index of tile, and in every view and layer there is an index of tile whose tiles receive exactly 8 from every owner, so that all their slots are used. `geometry`: components 0 and 1 are a splat's centre in pixels within its tile, from 0 to 32; components 2 and 3 lie in -0.5 to 2.0; component 4 in -0.6 to 0.6.
All inputs are finite; a program needn't handle non-finite values.
Results may differ from a plain program's by a relative error of at most 0.0073.
Values may be sent and summed in bfloat16 or wider, within the bound.
No kernel may reach another device: no remote copies, remote signals or barrier semaphores. Data moves between devices by JAX's collectives and lax.ppermute only.
A program may use at most 64 MiB of HBM per device.

v0:
```python
from functools import partial
import jax
import jax.numpy as jnp
from jax import lax
from jax.sharding import PartitionSpec as P

F = 128
W = 32
S = 128
VIEWS = 2
P_SIZE = 1024
clamp_top = 0.99
feature_rate = 0.5
opacity_rate = 0.5


def split_up(shard, dim, size):
    shape = shard.shape
    tiles = shard.reshape(*shape[:dim], size, shape[dim] // size, *shape[dim + 1 :])
    return jnp.moveaxis(tiles, dim, 0)


def sent_and_summed(shard, axis, dim):
    tiles = split_up(shard, dim, lax.axis_size(axis))
    arrived = lax.all_to_all(tiles, axis, split_axis=0, concat_axis=0, tiled=True)
    return arrived.astype(jnp.float32).sum(axis=0)


def joined_along(tiles, dim):
    tiles = jnp.moveaxis(tiles, 0, dim)
    shape = tiles.shape
    return tiles.reshape(*shape[:dim], shape[dim] * shape[dim + 1], *shape[dim + 2 :])


def from_everyone(shard, axis):
    copies = jnp.broadcast_to(shard, (lax.axis_size(axis), *shard.shape))
    return lax.all_to_all(copies, axis, split_axis=0, concat_axis=0, tiled=True)


def gather_directly(shard, axis, dim):
    return joined_along(from_everyone(shard, axis), dim)


def pixel_places():
    places = jnp.arange(P_SIZE, dtype=jnp.int32)
    across = (places % W).astype(jnp.float32) + 0.5
    downward = (places // W).astype(jnp.float32) + 0.5
    return (across, downward)


def block_sum(values, reverse):
    length = values.shape[0]
    block_rows = min(128, length)
    blocks = values.reshape(length // block_rows, block_rows, values.shape[1])
    positions = jnp.arange(block_rows)
    if reverse:
        triangle = (positions[:, None] < positions[None, :]).astype(jnp.float32)
    else:
        triangle = (positions[:, None] > positions[None, :]).astype(jnp.float32)
    within = jnp.einsum("ij,bjp->bip", triangle, blocks, precision=lax.Precision.HIGHEST)
    block_totals = jnp.sum(blocks, axis=1)
    if reverse:
        offsets = jnp.sum(block_totals, axis=0)[None, :] - jnp.cumsum(block_totals, axis=0)
    else:
        offsets = jnp.cumsum(block_totals, axis=0) - block_totals
    return (within + offsets[:, None, :]).reshape(length, values.shape[1])


def splat_fields(shapes):
    across, downward = pixel_places()
    delta_x = across[None, :] - shapes[0][:, None]
    delta_y = downward[None, :] - shapes[1][:, None]
    coef_a = jnp.exp(shapes[2])[:, None]
    coef_c = jnp.exp(shapes[3])[:, None]
    spread = jnp.exp(0.5 * (shapes[2] + shapes[3]))[:, None]
    coef_b = shapes[4][:, None] * spread
    quadric = (
        coef_a * delta_x * delta_x + 2.0 * coef_b * delta_x * delta_y + coef_c * delta_y * delta_y
    )
    falloff = jnp.exp(-0.5 * quadric)
    opacity = shapes[5][:, None]
    product = opacity * falloff
    coverage = jnp.minimum(product, clamp_top)
    return (delta_x, delta_y, coef_a, coef_b, coef_c, spread, falloff, opacity, product, coverage)


def layer_forward(inputs):
    slot_feats, shapes = inputs
    coverage = splat_fields(shapes)[9]
    log_keep = jnp.log(1.0 - coverage)
    before = block_sum(log_keep, False)
    weights = (coverage * jnp.exp(before)).astype(jnp.bfloat16)
    composite = lax.dot_general(
        slot_feats, weights, (((0,), (0,)), ((), ())), preferred_element_type=jnp.float32
    )
    layer_keep = jnp.exp(jnp.sum(log_keep, axis=0))
    return (composite, layer_keep)


def layer_backward(inputs):
    slot_feats, shapes, grad_comp, grad_keep = inputs
    delta_x, delta_y, coef_a, coef_b, coef_c, spread, falloff, opacity, product, coverage = (
        splat_fields(shapes)
    )
    log_keep = jnp.log(1.0 - coverage)
    before = block_sum(log_keep, False)
    decayed = jnp.exp(before)
    exact_weight = coverage * decayed
    weights = exact_weight.astype(jnp.bfloat16)
    layer_keep = jnp.exp(jnp.sum(log_keep, axis=0))
    grad_feat = lax.dot_general(
        weights, grad_comp, (((1,), (1,)), ((), ())), preferred_element_type=jnp.float32
    )
    grad_weight = jnp.dot(slot_feats, grad_comp, preferred_element_type=jnp.float32)
    grad_before = grad_weight * exact_weight
    later = block_sum(grad_before, True)
    grad_log = later + (grad_keep * layer_keep)[None, :]
    grad_coverage = grad_weight * decayed - grad_log / (1.0 - coverage)
    grad_product = jnp.where(product < clamp_top, grad_coverage, 0.0)
    grad_quadric = -0.5 * opacity * falloff * grad_product
    grad_mean_x = -2.0 * jnp.sum(grad_quadric * (coef_a * delta_x + coef_b * delta_y), axis=1)
    grad_mean_y = -2.0 * jnp.sum(grad_quadric * (coef_b * delta_x + coef_c * delta_y), axis=1)
    grad_first = jnp.sum(grad_quadric * delta_x * delta_x, axis=1)
    grad_cross = jnp.sum(grad_quadric * 2.0 * delta_x * delta_y, axis=1)
    grad_second = jnp.sum(grad_quadric * delta_y * delta_y, axis=1)
    grad_log_a = coef_a[:, 0] * grad_first + 0.5 * coef_b[:, 0] * grad_cross
    grad_log_c = coef_c[:, 0] * grad_second + 0.5 * coef_b[:, 0] * grad_cross
    grad_corr = spread[:, 0] * grad_cross
    opacity_flat = opacity[:, 0]
    grad_logit = opacity_flat * (1.0 - opacity_flat) * jnp.sum(falloff * grad_product, axis=1)
    grad_shape = jnp.stack(
        [grad_mean_x, grad_mean_y, grad_log_a, grad_log_c, grad_corr, grad_logit]
    )
    return (grad_feat, grad_shape)


def rear_step(all_keeps, all_terms, depth_here, layers, counter, carried):
    layer_at = layers - 1 - counter
    updated = all_terms[layer_at] + all_keeps[layer_at] * carried
    return jnp.where(layer_at > depth_here, updated, carried)


def body(features, logits, geometry, dest_slot, target):
    owners = lax.axis_size("tile")
    layers = lax.axis_size("depth")
    depth_here = lax.axis_index("depth")
    tiles_here = target.shape[1]
    owned = features.shape[1]
    capacity = owned // owners
    pixel_share = P_SIZE // layers
    splat_feats = features[0]
    logit_now = logits[0]
    images = []
    shape_grads = []
    for view_index in range(VIEWS):
        slot_ids = dest_slot[view_index, 0]
        visible = slot_ids >= 0
        receiver = jnp.where(visible, slot_ids // owned, owners)
        matches = (receiver[:, None] == jnp.arange(owners, dtype=jnp.int32)[None, :]).astype(
            jnp.int32
        )
        place_in = jnp.sum((jnp.cumsum(matches, axis=0) - matches) * matches, axis=1)
        position = jnp.where(visible, receiver * capacity + place_in, owners * capacity)
        local_slot = jnp.where(visible, slot_ids - receiver * owned, -1)
        opacity = jax.nn.sigmoid(logit_now)
        shape_rows = jnp.concatenate([geometry[view_index, 0], opacity[None, :]], axis=0).T
        row_buffer = (
            jnp.zeros((owners * capacity + 1, F), jnp.bfloat16)
            .at[position]
            .set(splat_feats)[:-1]
            .reshape(owners, capacity, F)
        )
        slot_buffer = (
            jnp.full((owners * capacity + 1,), -1, jnp.int32)
            .at[position]
            .set(local_slot)[:-1]
            .reshape(owners, capacity)
        )
        shape_buffer = (
            jnp.zeros((owners * capacity + 1, 6), jnp.float32)
            .at[position]
            .set(shape_rows)[:-1]
            .reshape(owners, capacity, 6)
        )
        got_rows, got_slots = (
            lax.all_to_all(row_buffer, "tile", split_axis=0, concat_axis=0, tiled=True),
            lax.all_to_all(slot_buffer, "tile", split_axis=0, concat_axis=0, tiled=True),
        )
        got_shapes = lax.all_to_all(shape_buffer, "tile", split_axis=0, concat_axis=0, tiled=True)
        arrived = got_slots.reshape(-1)
        present = arrived >= 0
        landing = jnp.where(present, arrived, owned)
        slot_feats = (
            jnp.zeros((owned + 1, F), jnp.bfloat16)
            .at[landing]
            .set(got_rows.reshape(-1, F))[:-1]
            .reshape(tiles_here, S, F)
        )
        slot_shapes = (
            jnp.zeros((owned + 1, 6), jnp.float32)
            .at[landing]
            .set(got_shapes.reshape(-1, 6))[:-1]
            .reshape(tiles_here, S, 6)
            .transpose(0, 2, 1)
        )
        composites, layer_keeps = lax.map(layer_forward, (slot_feats, slot_shapes))
        all_keeps = lax.all_gather(layer_keeps[None], "depth", axis=0, tiled=True)
        earlier_mask = (jnp.arange(layers) < depth_here)[:, None, None]
        ahead = jnp.prod(jnp.where(earlier_mask, all_keeps, 1.0), axis=0)
        contrib = ahead[:, None, :] * composites
        image_part = sent_and_summed(contrib.astype(jnp.bfloat16), "depth", 2)
        target_part = lax.dynamic_slice_in_dim(
            target[view_index], depth_here * pixel_share, pixel_share, 2
        ).astype(jnp.float32)
        residual = gather_directly(image_part - target_part, "depth", 2)
        images.append(image_part.astype(jnp.bfloat16))
        pixel_terms = jnp.sum(residual * composites, axis=1)
        all_terms = gather_directly(pixel_terms[None], "depth", 0)
        behind = lax.fori_loop(
            0,
            layers,
            partial(rear_step, all_keeps, all_terms, depth_here, layers),
            jnp.zeros_like(pixel_terms),
        )
        grad_keep = ahead * behind
        grad_comp = (ahead[:, None, :] * residual).astype(jnp.bfloat16)
        grad_feat, grad_shape = lax.map(
            layer_backward, (slot_feats, slot_shapes, grad_comp, grad_keep)
        )
        flat_feat = grad_feat.reshape(owned, F)
        flat_shape = grad_shape.transpose(0, 2, 1).reshape(owned, 6)
        fetched = jnp.where(present, arrived, 0)
        back_feat = jnp.where(present[:, None], flat_feat[fetched], 0.0).reshape(
            owners, capacity, F
        )
        back_shape = jnp.where(present[:, None], flat_shape[fetched], 0.0).reshape(
            owners, capacity, 6
        )
        return_feat, return_shape = (
            lax.all_to_all(back_feat, "tile", split_axis=0, concat_axis=0, tiled=True),
            lax.all_to_all(back_shape, "tile", split_axis=0, concat_axis=0, tiled=True),
        )
        padded_feat = jnp.concatenate(
            [return_feat.reshape(-1, F), jnp.zeros((1, F), jnp.float32)], axis=0
        )
        padded_shape = jnp.concatenate(
            [return_shape.reshape(-1, 6), jnp.zeros((1, 6), jnp.float32)], axis=0
        )
        splat_grad_feat = padded_feat[position]
        splat_grad_shape = padded_shape[position]
        shape_grads.append(splat_grad_shape[:, :5].T)
        splat_feats = (splat_feats.astype(jnp.float32) - feature_rate * splat_grad_feat).astype(
            jnp.bfloat16
        )
        logit_now = logit_now - opacity_rate * splat_grad_shape[:, 5]
    return (jnp.stack(images), splat_feats[None], logit_now[None], jnp.stack(shape_grads)[:, None])


def solution(mesh):
    placed = (
        P("depth", "tile", None),
        P("depth", "tile"),
        P(None, "depth", None, "tile"),
        P(None, "depth", "tile"),
        P(None, "tile", None, None),
    )
    return jax.shard_map(
        body,
        mesh=mesh,
        in_specs=placed,
        out_specs=(
            P(None, "tile", None, "depth"),
            P("depth", "tile", None),
            P("depth", "tile"),
            P(None, "depth", None, "tile"),
        ),
        check_vma=False,
    )
```

profile of v0, /device:TPU:1, one launch (start us, length us, event | category | flops | bytes accessed | tf_op | source)
XLA Modules:
  0.0 448.0 jit_solution(14896957817625969627)
XLA Ops:
  6.5 1.4 scatter_custom_fusion
  8.6 10.4 %all-to-all-start = ((s32[32,1,8]{2,1,0:T(1,128)}), s32[32,1,8]{2,1,0:T(1,128)S(1)}, u32[]{:S(2)}, u32[]{:S(2)}) async-start(s32[32,1,8]{2,1,0:T(1,128)} %bitcast.92), calls=%async_computation | async-start | bytes 32768 | tf_op jit(solution)/shard_map/all_to_all | solution.py:187
  19.9 1.2 scatter_custom_fusion.3
  21.9 1.2 scatter_custom_fusion.1
  23.8 2.3 all-to-all-done
  26.1 5.2 %all-to-all-start.2 = ((f32[32,8,6]{2,1,0:T(8,128)}), f32[32,8,6]{2,1,0:T(8,128)S(1)}, u32[]{:S(2)}, u32[]{:S(2)}) async-start(f32[32,8,6]{2,1,0:T(8,128)} %slice_bitcast_fusion.15), calls=%async_computation.2 | async-start | bytes 262144 | tf_op jit(solution)/shard_map/all_to_all | solution.py:189
  32.6 6.3 %all-to-all-done.2 = f32[32,8,6]{2,1,0:T(8,128)S(1)} async-done(((f32[32,8,6]{2,1,0:T(8,128)}), f32[32,8,6]{2,1,0:T(8,128)S(1)}, u32[]{:S(2)}, u32[]{:S(2)}) %all-to-all-start.2) | async-done | bytes 6176 | tf_op jit(solution)/shard_map/all_to_all | solution.py:189
  38.9 3.9 all-to-all-start.1
  42.8 1.2 scatter_custom_fusion.4
  44.1 6.2 %all-to-all-done.1 = bf16[32,8,128]{2,1,0:T(8,128)(2,1)S(1)} async-done(((bf16[32,8,128]{2,1,0:T(8,128)(2,1)}), bf16[32,8,128]{2,1,0:T(8,128)(2,1)S(1)}, u32[]{:S(2)}, u32[]{:S(2)}) %all-to-all-start.1) | async-done | bytes 65568 | tf_op jit(solution)/shard_map/all_to_all | solution.py:186
  50.2 1.2 scatter_custom_fusion.2
  52.9 5.0 %while.88 = (s32[]{:T(128)}, f32[2,128,1024]{1,2,0:T(8,128)S(1)}, f32[2,1024]{1,0:T(2,128)S(1)}, bf16[2,128,128]{2,1,0:T(8,128)(2,1)S(1)}, f32[2,6,128]{2,1,0:T(8,128)S(1)}, /*index=5*/s32[]{:T(128)}, s32[]{:T(128)}) while((s32[]{:T(128)}, f32[2,128,1024]{1,2,0:T(8,128)S(1)}, f32[2,1024]{1,0:T(2,128)S(1)}, ...), condition=%wide.region_11.12_spmd, body=%wide.region_8.11_spmd.sunk | while | flops 242777600 | bytes 1177685 | solution.py:206
  53.4 1.2 fusion.322
  55.9 1.2 fusion.322
  57.9 27.0 %all-gather.2 = f32[16,2,1024]{2,1,0:T(2,128)S(1)} all-gather(f32[1,2,1024]{2,1,0:T(2,128)S(1)} %bitcast.719), channel_id=2, replica_groups=mesh['tile'=32,'depth'=16] {'depth'}, dimensions={0}, use_global_device_ids=true | all-gather | bytes 139264 | tf_op jit(solution)/shard_map/all_gather | solution.py:207
  85.4 0.8 copy.118
  86.2 6.7 %all-to-all-start.3 = ((bf16[16,2,128,64]{2,3,1,0:T(8,128)(2,1)}), bf16[16,2,128,64]{2,3,1,0:T(8,128)(2,1)S(1)}, u32[]{:S(2)}, u32[]{:S(2)}) async-start(bf16[16,2,128,64]{2,3,1,0:T(8,128)(2,1)} %copy.118), calls=%async_computation.3 | async-start | bytes 1048576 | tf_op jit(solution)/shard_map/all_to_all | solution.py:25
  93.2 18.2 %all-to-all-done.3 = bf16[16,2,128,64]{2,3,1,0:T(8,128)(2,1)S(1)} async-done(((bf16[16,2,128,64]{2,3,1,0:T(8,128)(2,1)}), bf16[16,2,128,64]{2,3,1,0:T(8,128)(2,1)S(1)}, u32[]{:S(2)}, u32[]{:S(2)}) %all-to-all-start.3) | async-done | bytes 524320 | tf_op jit(solution)/shard_map/all_to_all | solution.py:25
  111.6 1.1 broadcast_in_dim.232
  112.7 13.6 %all-to-all-start.5 = ((f32[16,2,128,64]{2,3,1,0:T(8,128)}), f32[16,2,128,64]{2,3,1,0:T(8,128)S(1)}, u32[]{:S(2)}, u32[]{:S(2)}) async-start(f32[16,2,128,64]{2,3,1,0:T(8,128)} %broadcast_in_dim.232), calls=%async_computation.5 | async-start | bytes 2097152 | tf_op jit(solution)/shard_map/all_to_all | solution.py:37
  126.3 1.4 scatter_custom_fusion.5
  128.4 42.7 %all-to-all-done.5 = f32[16,2,128,64]{2,3,1,0:T(8,128)S(1)} async-done(((f32[16,2,128,64]{2,3,1,0:T(8,128)}), f32[16,2,128,64]{2,3,1,0:T(8,128)S(1)}, u32[]{:S(2)}, u32[]{:S(2)}) %all-to-all-start.5) | async-done | bytes 1048608 | tf_op jit(solution)/shard_map/all_to_all | solution.py:37
  171.1 8.5 %all-to-all-start.4 = ((s32[32,1,8]{2,1,0:T(1,128)}), s32[32,1,8]{2,1,0:T(1,128)S(1)}, u32[]{:S(2)}, u32[]{:S(2)}) async-start(s32[32,1,8]{2,1,0:T(1,128)} %bitcast.113), calls=%async_computation.4 | async-start | bytes 32768 | tf_op jit(solution)/shard_map/all_to_all | solution.py:187
  180.4 6.2 %all-to-all-done.4 = s32[32,1,8]{2,1,0:T(1,128)S(1)} async-done(((s32[32,1,8]{2,1,0:T(1,128)}), s32[32,1,8]{2,1,0:T(1,128)S(1)}, u32[]{:S(2)}, u32[]{:S(2)}) %all-to-all-start.4) | async-done | bytes 1056 | tf_op jit(solution)/shard_map/all_to_all | solution.py:187
  187.3 8.8 %all-to-all-start.6 = ((f32[16,1,2,1024]{3,2,1,0:T(2,128)}), f32[16,1,2,1024]{3,2,1,0:T(2,128)S(1)}, u32[]{:S(2)}, u32[]{:S(2)}) async-start(f32[16,1,2,1024]{3,2,1,0:T(2,128)} %broadcast_in_dim.233), calls=%async_computation.6 | async-start | bytes 262144 | tf_op jit(solution)/shard_map/all_to_all | solution.py:37
  197.1 11.0 %all-to-all-done.6 = f32[16,1,2,1024]{3,2,1,0:T(2,128)S(1)} async-done(((f32[16,1,2,1024]{3,2,1,0:T(2,128)}), f32[16,1,2,1024]{3,2,1,0:T(2,128)S(1)}, u32[]{:S(2)}, u32[]{:S(2)}) %all-to-all-start.6) | async-done | bytes 131104 | tf_op jit(solution)/shard_map/all_to_all | solution.py:37
  208.1 0.8 while.92
  209.0 9.3 %while.89 = (s32[]{:T(128)}, f32[2,128,128]{2,1,0:T(8,128)S(1)}, f32[2,6,128]{2,1,0:T(8,128)S(1)}, f32[2,6,128]{2,1,0:T(8,128)S(1)}, bf16[2,128,1024]{1,2,0:T(8,...) while((s32[]{:T(128)}, f32[2,128,128]{2,1,0:T(8,128)S(1)}, ...), condition=%wide.region_31.32_spmd, body=%wide.region_21.31_spmd.sunk | while | flops 485672448 | bytes 3947105 | solution.py:227
  211.0 1.9 fusion.332
  215.7 1.9 fusion.332
  219.1 0.8 bitcast_select_fusion.2
  219.9 7.2 %all-to-all-start.9 = ((f32[32,8,6]{2,1,0:T(8,128)}), f32[32,8,6]{2,1,0:T(8,128)S(1)}, u32[]{:S(2)}, u32[]{:S(2)}) async-start(f32[32,8,6]{2,1,0:T(8,128)} %bitcast_select_fusion.2), calls=%async_computation.9 | async-start | bytes 262144 | tf_op jit(solution)/shard_map/all_to_all | solution.py:241
  228.6 6.2 %all-to-all-done.9 = f32[32,8,6]{2,1,0:T(8,128)S(1)} async-done(((f32[32,8,6]{2,1,0:T(8,128)}), f32[32,8,6]{2,1,0:T(8,128)S(1)}, u32[]{:S(2)}, u32[]{:S(2)}) %all-to-all-start.9) | async-done | bytes 6176 | tf_op jit(solution)/shard_map/all_to_all | solution.py:241
  234.8 3.9 all-to-all-start.7
  239.9 1.2 scatter_custom_fusion.8
  241.7 4.8 %all-to-all-done.7 = f32[32,8,128]{2,1,0:T(8,128)S(1)} async-done(((f32[32,8,128]{2,1,0:T(8,128)}), f32[32,8,128]{2,1,0:T(8,128)S(1)}, u32[]{:S(2)}, u32[]{:S(2)}) %all-to-all-start.7) | async-done | bytes 131104 | tf_op jit(solution)/shard_map/all_to_all | solution.py:240
  246.5 3.9 all-to-all-start.10
  251.1 1.2 scatter_custom_fusion.6
  253.0 5.1 %all-to-all-done.10 = f32[32,8,6]{2,1,0:T(8,128)S(1)} async-done(((f32[32,8,6]{2,1,0:T(8,128)}), f32[32,8,6]{2,1,0:T(8,128)S(1)}, u32[]{:S(2)}, u32[]{:S(2)}) %all-to-all-start.10) | async-done | bytes 6176 | tf_op jit(solution)/shard_map/all_to_all | solution.py:189
  258.1 3.9 all-to-all-start.8
  262.0 1.2 scatter_custom_fusion.9
  263.3 6.2 %all-to-all-done.8 = bf16[32,8,128]{2,1,0:T(8,128)(2,1)S(1)} async-done(((bf16[32,8,128]{2,1,0:T(8,128)(2,1)}), bf16[32,8,128]{2,1,0:T(8,128)(2,1)S(1)}, u32[]{:S(2)}, u32[]{:S(2)}) %all-to-all-start.8) | async-done | bytes 65568 | tf_op jit(solution)/shard_map/all_to_all | solution.py:186
  269.4 1.2 scatter_custom_fusion.7
  272.1 5.0 %while.90 = (s32[]{:T(128)}, f32[2,128,1024]{1,2,0:T(8,128)S(1)}, f32[2,1024]{1,0:T(2,128)S(1)}, bf16[2,128,128]{2,1,0:T(8,128)(2,1)S(1)}, f32[2,6,128]{2,1,0:T(8,128)S(1)}, /*index=5*/s32[]{:T(128)}, s32[]{:T(128)}) while((s32[]{:T(128)}, f32[2,128,1024]{1,2,0:T(8,128)S(1)}, f32[2,1024]{1,0:T(2,128)S(1)}, ...), condition=%wide.region_39.40_spmd, body=%wide.region_36.39_spmd.sunk | while | flops 242777600 | bytes 1177685 | solution.py:206
  272.6 1.2 fusion.338
  275.2 1.2 fusion.338
  277.1 21.9 %all-gather.3 = f32[16,2,1024]{2,1,0:T(2,128)S(1)} all-gather(f32[1,2,1024]{2,1,0:T(2,128)S(1)} %bitcast.721), channel_id=3, replica_groups=mesh['tile'=32,'depth'=16] {'depth'}, dimensions={0}, use_global_device_ids=true | all-gather | bytes 139264 | tf_op jit(solution)/shard_map/all_gather | solution.py:207
  299.5 0.8 copy.132
  300.3 4.1 all-to-all-start.11
  304.6 18.2 %all-to-all-done.11 = bf16[16,2,128,64]{2,3,1,0:T(8,128)(2,1)S(1)} async-done(((bf16[16,2,128,64]{2,3,1,0:T(8,128)(2,1)}), bf16[16,2,128,64]{2,3,1,0:T(8,128)(2,1)S(1)}, u32[]{:S(2)}, u32[]{:S(2)}) %all-to-all-start.11) | async-done | bytes 524320 | tf_op jit(solution)/shard_map/all_to_all | solution.py:25
  322.9 1.1 broadcast_in_dim.239
  324.0 13.6 %all-to-all-start.12 = ((f32[16,2,128,64]{2,3,1,0:T(8,128)}), f32[16,2,128,64]{2,3,1,0:T(8,128)S(1)}, u32[]{:S(2)}, u32[]{:S(2)}) async-start(f32[16,2,128,64]{2,3,1,0:T(8,128)} %broadcast_in_dim.239), calls=%async_computation.12 | async-start | bytes 2097152 | tf_op jit(solution)/shard_map/all_to_all | solution.py:37
  337.7 44.8 %all-to-all-done.12 = f32[16,2,128,64]{2,3,1,0:T(8,128)S(1)} async-done(((f32[16,2,128,64]{2,3,1,0:T(8,128)}), f32[16,2,128,64]{2,3,1,0:T(8,128)S(1)}, u32[]{:S(2)}, u32[]{:S(2)}) %all-to-all-start.12) | async-done | bytes 1048608 | tf_op jit(solution)/shard_map/all_to_all | solution.py:37
  383.9 12.4 %all-to-all-start.13 = ((f32[16,1,2,1024]{3,2,1,0:T(2,128)}), f32[16,1,2,1024]{3,2,1,0:T(2,128)S(1)}, u32[]{:S(2)}, u32[]{:S(2)}) async-start(f32[16,1,2,1024]{3,2,1,0:T(2,128)} %broadcast_in_dim.240), calls=%async_computation.13 | async-start | bytes 262144 | tf_op jit(solution)/shard_map/all_to_all | solution.py:37
  397.2 11.1 %all-to-all-done.13 = f32[16,1,2,1024]{3,2,1,0:T(2,128)S(1)} async-done(((f32[16,1,2,1024]{3,2,1,0:T(2,128)}), f32[16,1,2,1024]{3,2,1,0:T(2,128)S(1)}, u32[]{:S(2)}, u32[]{:S(2)}) %all-to-all-start.13) | async-done | bytes 131104 | tf_op jit(solution)/shard_map/all_to_all | solution.py:37
  408.3 0.8 while.93
  409.2 9.1 %while.91 = (s32[]{:T(128)}, f32[2,128,128]{2,1,0:T(8,128)S(1)}, f32[2,6,128]{2,1,0:T(8,128)S(1)}, f32[2,6,128]{2,1,0:T(8,128)S(1)}, bf16[2,128,1024]{1,2,0:T(8,...) while((s32[]{:T(128)}, f32[2,128,128]{2,1,0:T(8,128)S(1)}, ...), condition=%wide.region_55.56_spmd, body=%wide.region_45.55_spmd.sunk | while | flops 485672448 | bytes 3947105 | solution.py:227
  411.2 1.9 fusion.348
  415.8 1.9 fusion.348
  419.2 0.8 bitcast_select_fusion
  419.9 7.3 %all-to-all-start.15 = ((f32[32,8,6]{2,1,0:T(8,128)}), f32[32,8,6]{2,1,0:T(8,128)S(1)}, u32[]{:S(2)}, u32[]{:S(2)}) async-start(f32[32,8,6]{2,1,0:T(8,128)} %bitcast_select_fusion), calls=%async_computation.15 | async-start | bytes 262144 | tf_op jit(solution)/shard_map/all_to_all | solution.py:241
  428.7 6.2 %all-to-all-done.15 = f32[32,8,6]{2,1,0:T(8,128)S(1)} async-done(((f32[32,8,6]{2,1,0:T(8,128)}), f32[32,8,6]{2,1,0:T(8,128)S(1)}, u32[]{:S(2)}, u32[]{:S(2)}) %all-to-all-start.15) | async-done | bytes 6176 | tf_op jit(solution)/shard_map/all_to_all | solution.py:241
  434.9 3.9 all-to-all-start.14
  441.1 5.5 %all-to-all-done.14 = f32[32,8,128]{2,1,0:T(8,128)S(1)} async-done(((f32[32,8,128]{2,1,0:T(8,128)}), f32[32,8,128]{2,1,0:T(8,128)S(1)}, u32[]{:S(2)}, u32[]{:S(2)}) %all-to-all-start.14) | async-done | bytes 131104 | tf_op jit(solution)/shard_map/all_to_all | solution.py:240
  (274 shorter events, 47.4 us)
Async XLA Ops:
  2.2 0.6 copy-start.6
  3.6 0.6 copy-start.7
  4.2 0.7 slice-start.2
  5.0 0.7 slice-start.3
  5.8 0.7 copy-start.5
  8.6 10.5 %copy-start.4 = (f32[2,1,5,256]{3,1,2,0:T(1,128)S(1)}, f32[2,1,5,256]{3,1,2,0:T(1,128)}, u32[]{:S(2)}) copy-start(f32[2,1,5,256]{3,1,2,0:T(1,128)} %param.19) | copy-start | bytes 30724
  8.6 17.5 %all-to-all-start = ((s32[32,1,8]{2,1,0:T(1,128)}), s32[32,1,8]{2,1,0:T(1,128)S(1)}, u32[]{:S(2)}, u32[]{:S(2)}) async-start(s32[32,1,8]{2,1,0:T(1,128)} %bitcast.92), calls=%async_computation | async-start | bytes 32768 | tf_op jit(solution)/shard_map/all_to_all | solution.py:187
  19.1 0.7 copy-start.8
  21.1 0.8 copy-start.3
  26.1 12.8 %all-to-all-start.2 = ((f32[32,8,6]{2,1,0:T(8,128)}), f32[32,8,6]{2,1,0:T(8,128)S(1)}, u32[]{:S(2)}, u32[]{:S(2)}) async-start(f32[32,8,6]{2,1,0:T(8,128)} %slice_bitcast_fusion.15), calls=%async_computation.2 | async-start | bytes 262144 | tf_op jit(solution)/shard_map/all_to_all | solution.py:189
  38.9 11.4 %all-to-all-start.1 = ((bf16[32,8,128]{2,1,0:T(8,128)(2,1)}), bf16[32,8,128]{2,1,0:T(8,128)(2,1)S(1)}, u32[]{:S(2)}, u32[]{:S(2)}) async-start(bf16[32,8,128]{2,1,0:T(8,128)(2,1)} %slice_bitcast_fusion.17), calls=%async_computation.1 | async-start | bytes 131072 | tf_op jit(solution)/shard_map/all_to_all | solution.py:186
  51.4 0.6 copy-start.1
  52.0 0.8 slice-start
  85.4 7.6 %copy-start = (bf16[2,2,128,1024]{3,2,1,0:T(8,128)(2,1)S(1)}, bf16[2,2,128,1024]{3,2,1,0:T(8,128)(2,1)}, u32[]{:S(2)}) copy-start(bf16[2,2,128,1024]{3,2,1,0:T(8,128)(2,1)} %param.21) | copy-start | bytes 3145732
  86.2 25.2 %all-to-all-start.3 = ((bf16[16,2,128,64]{2,3,1,0:T(8,128)(2,1)}), bf16[16,2,128,64]{2,3,1,0:T(8,128)(2,1)S(1)}, u32[]{:S(2)}, u32[]{:S(2)}) async-start(bf16[16,2,128,64]{2,3,1,0:T(8,128)(2,1)} %copy.118), calls=%async_computation.3 | async-start | bytes 1048576 | tf_op jit(solution)/shard_map/all_to_all | solution.py:25
  112.7 58.4 %all-to-all-start.5 = ((f32[16,2,128,64]{2,3,1,0:T(8,128)}), f32[16,2,128,64]{2,3,1,0:T(8,128)S(1)}, u32[]{:S(2)}, u32[]{:S(2)}) async-start(f32[16,2,128,64]{2,3,1,0:T(8,128)} %broadcast_in_dim.232), calls=%async_computation.5 | async-start | bytes 2097152 | tf_op jit(solution)/shard_map/all_to_all | solution.py:37
  171.1 15.5 %all-to-all-start.4 = ((s32[32,1,8]{2,1,0:T(1,128)}), s32[32,1,8]{2,1,0:T(1,128)S(1)}, u32[]{:S(2)}, u32[]{:S(2)}) async-start(s32[32,1,8]{2,1,0:T(1,128)} %bitcast.113), calls=%async_computation.4 | async-start | bytes 32768 | tf_op jit(solution)/shard_map/all_to_all | solution.py:187
  187.3 20.8 %all-to-all-start.6 = ((f32[16,1,2,1024]{3,2,1,0:T(2,128)}), f32[16,1,2,1024]{3,2,1,0:T(2,128)S(1)}, u32[]{:S(2)}, u32[]{:S(2)}) async-start(f32[16,1,2,1024]{3,2,1,0:T(2,128)} %broadcast_in_dim.233), calls=%async_computation.6 | async-start | bytes 262144 | tf_op jit(solution)/shard_map/all_to_all | solution.py:37
  219.9 15.0 %all-to-all-start.9 = ((f32[32,8,6]{2,1,0:T(8,128)}), f32[32,8,6]{2,1,0:T(8,128)S(1)}, u32[]{:S(2)}, u32[]{:S(2)}) async-start(f32[32,8,6]{2,1,0:T(8,128)} %bitcast_select_fusion.2), calls=%async_computation.9 | async-start | bytes 262144 | tf_op jit(solution)/shard_map/all_to_all | solution.py:241
  234.8 11.6 %all-to-all-start.7 = ((f32[32,8,128]{2,1,0:T(8,128)}), f32[32,8,128]{2,1,0:T(8,128)S(1)}, u32[]{:S(2)}, u32[]{:S(2)}) async-start(f32[32,8,128]{2,1,0:T(8,128)} %bitcast_select_fusion.3), calls=%async_computation.7 | async-start | bytes 262144 | tf_op jit(solution)/shard_map/all_to_all | solution.py:240
  246.5 11.6 %all-to-all-start.10 = ((f32[32,8,6]{2,1,0:T(8,128)}), f32[32,8,6]{2,1,0:T(8,128)S(1)}, u32[]{:S(2)}, u32[]{:S(2)}) async-start(f32[32,8,6]{2,1,0:T(8,128)} %slice_bitcast_fusion.14), calls=%async_computation.10 | async-start | bytes 262144 | tf_op jit(solution)/shard_map/all_to_all | solution.py:189
  258.1 11.4 %all-to-all-start.8 = ((bf16[32,8,128]{2,1,0:T(8,128)(2,1)}), bf16[32,8,128]{2,1,0:T(8,128)(2,1)S(1)}, u32[]{:S(2)}, u32[]{:S(2)}) async-start(bf16[32,8,128]{2,1,0:T(8,128)(2,1)} %slice_bitcast_fusion.16), calls=%async_computation.8 | async-start | bytes 131072 | tf_op jit(solution)/shard_map/all_to_all | solution.py:186
  270.6 0.6 copy-start.2
  271.3 0.8 slice-start.1
  300.3 22.5 %all-to-all-start.11 = ((bf16[16,2,128,64]{2,3,1,0:T(8,128)(2,1)}), bf16[16,2,128,64]{2,3,1,0:T(8,128)(2,1)S(1)}, u32[]{:S(2)}, u32[]{:S(2)}) async-start(bf16[16,2,128,64]{2,3,1,0:T(8,128)(2,1)} %copy.132), calls=%async_computation.11 | async-start | bytes 1048576 | tf_op jit(solution)/shard_map/all_to_all | solution.py:25
  324.0 58.5 %all-to-all-start.12 = ((f32[16,2,128,64]{2,3,1,0:T(8,128)}), f32[16,2,128,64]{2,3,1,0:T(8,128)S(1)}, u32[]{:S(2)}, u32[]{:S(2)}) async-start(f32[16,2,128,64]{2,3,1,0:T(8,128)} %broadcast_in_dim.239), calls=%async_computation.12 | async-start | bytes 2097152 | tf_op jit(solution)/shard_map/all_to_all | solution.py:37
  383.9 24.4 %all-to-all-start.13 = ((f32[16,1,2,1024]{3,2,1,0:T(2,128)}), f32[16,1,2,1024]{3,2,1,0:T(2,128)S(1)}, u32[]{:S(2)}, u32[]{:S(2)}) async-start(f32[16,1,2,1024]{3,2,1,0:T(2,128)} %broadcast_in_dim.240), calls=%async_computation.13 | async-start | bytes 262144 | tf_op jit(solution)/shard_map/all_to_all | solution.py:37
  419.9 15.0 %all-to-all-start.15 = ((f32[32,8,6]{2,1,0:T(8,128)}), f32[32,8,6]{2,1,0:T(8,128)S(1)}, u32[]{:S(2)}, u32[]{:S(2)}) async-start(f32[32,8,6]{2,1,0:T(8,128)} %bitcast_select_fusion), calls=%async_computation.15 | async-start | bytes 262144 | tf_op jit(solution)/shard_map/all_to_all | solution.py:241
  434.9 11.6 %all-to-all-start.14 = ((f32[32,8,128]{2,1,0:T(8,128)}), f32[32,8,128]{2,1,0:T(8,128)S(1)}, u32[]{:S(2)}, u32[]{:S(2)}) async-start(f32[32,8,128]{2,1,0:T(8,128)} %bitcast_select_fusion.1), calls=%async_computation.14 | async-start | bytes 262144 | tf_op jit(solution)/shard_map/all_to_all | solution.py:240
where the time goes:
time: 450 us; the launch traced here: 448 us
  waiting for transfers between devices  201 us (45%)
  starting transfers between devices  118 us (26%)
  blocking collectives  48.9 us (11%)
  local copies, waits for them, and re-layouts  37.7 us (8%)
  matrix products  21.2 us (5%)
  other arithmetic  18.5 us (4%)
    all_to_all x4, waiting for transfers between devices, from_everyone(): return lax.all_to_all(copies, axis, split_axis=0, concat_axis=0, tiled=True)  110 us
    all_gather x2, blocking collectives, body(): all_keeps = lax.all_gather(layer_keeps[None], 'depth', axis=0, tiled=True)  48.9 us
    all_to_all x4, starting transfers between devices, from_everyone(): return lax.all_to_all(copies, axis, split_axis=0, concat_axis=0, tiled=True)  48.4 us
    all_to_all x2, waiting for transfers between devices, sent_and_summed(): lax.all_to_all(tiles, axis, split_axis=0, concat_axis=0, tiled=True)  36.4 us
    all_to_all x2, starting transfers between devices, body(): lax.all_to_all(slot_buffer, 'tile', split_axis=0, concat_axis=0, tiled=True)  19 us
    dot_general x12, matrix products, block_sum(): jnp.einsum('ij,bjp->bip', triangle, blocks, precision=lax.Precision.HIGHEST)  15.4 us
    all_to_all x2, starting transfers between devices, body(): lax.all_to_all(back_shape, 'tile', split_axis=0, concat_axis=0, tiled=True)  14.5 us
    all_to_all x2, waiting for transfers between devices, body(): lax.all_to_all(back_shape, 'tile', split_axis=0, concat_axis=0, tiled=True)  12.5 us
  transfers between devices with their start and end apart: 16, of which 16 were waited for; matrix products, arithmetic and copies ran while one was open for 5% of the time, Pallas kernels for 0%

commit v1 on v0

--- a/solution.py
+++ b/solution.py
@@ -204,7 +204,10 @@
             .transpose(0, 2, 1)
         )
         composites, layer_keeps = lax.map(layer_forward, (slot_feats, slot_shapes))
-        all_keeps = lax.all_gather(layer_keeps[None], "depth", axis=0, tiled=True)
+        all_keeps = jnp.concatenate(
+            lax.all_to_all(jnp.stack([layer_keeps[None]] * lax.axis_size("depth")), "depth", 0, 0),
+            axis=0,
+        )
         earlier_mask = (jnp.arange(layers) < depth_here)[:, None, None]
         ahead = jnp.prod(jnp.where(earlier_mask, all_keeps, 1.0), axis=0)
         contrib = ahead[:, None, :] * composites

time: 450 us -> 451 us (level)
  blocking collectives: 48.9 us -> 15.4 us
  waiting for transfers between devices: 201 us -> 223 us
  starting transfers between devices: 118 us -> 129 us
    all_gather x2 -> x0, blocking collectives: 48.9 us -> none  [body(): all_keeps = lax.all_gather(layer_keeps[None], 'depth', axis=0, tiled=True)]
    all_to_all x0 -> x1, blocking collectives: none -> 15.4 us  [body(): lax.all_to_all(jnp.stack([layer_keeps[None]] * lax.axis_size('depth')), '...]
    all_to_all x0 -> x1, starting transfers between devices: none -> 13.1 us  [body(): lax.all_to_all(jnp.stack([layer_keeps[None]] * lax.axis_size('depth')), '...]
    all_to_all x0 -> x1, waiting for transfers between devices: none -> 12.1 us  [body(): lax.all_to_all(jnp.stack([layer_keeps[None]] * lax.axis_size('depth')), '...]
    all_to_all x2, waiting for transfers between devices: 36.4 us -> 45.4 us  [sent_and_summed(): lax.all_to_all(tiles, axis, split_axis=0, concat_axis=0, tiled=True)]
  transfers between devices with their start and end apart: 16 -> 17, of which waited for: 16 -> 17; matrix products, arithmetic and copies ran while one was open for 5% -> 5% of each run, Pallas kernels for 0% -> 0%
where the time goes in v1:
time: 451 us; the launch traced here: 449 us
  waiting for transfers between devices  223 us (49%)
  starting transfers between devices  129 us (29%)
  local copies, waits for them, and re-layouts  38.7 us (9%)
  matrix products  21.2 us (5%)
  other arithmetic  18.5 us (4%)
  blocking collectives  15.4 us (3%)
    all_to_all x4, waiting for transfers between devices, from_everyone(): return lax.all_to_all(copies, axis, split_axis=0, concat_axis=0, tiled=True)  110 us
    all_to_all x4, starting transfers between devices, from_everyone(): return lax.all_to_all(copies, axis, split_axis=0, concat_axis=0, tiled=True)  45.5 us
    all_to_all x2, waiting for transfers between devices, sent_and_summed(): lax.all_to_all(tiles, axis, split_axis=0, concat_axis=0, tiled=True)  45.4 us
    all_to_all x2, starting transfers between devices, body(): lax.all_to_all(slot_buffer, 'tile', split_axis=0, concat_axis=0, tiled=True)  19.7 us
    dot_general x12, matrix products, block_sum(): jnp.einsum('ij,bjp->bip', triangle, blocks, precision=lax.Precision.HIGHEST)  15.4 us
    all_to_all x1, blocking collectives, body(): lax.all_to_all(jnp.stack([layer_keeps[None]] * lax.axis_size('depth')), '...  15.4 us
    all_to_all x2, starting transfers between devices, body(): lax.all_to_all(back_shape, 'tile', split_axis=0, concat_axis=0, tiled=True)  14.1 us
    all_to_all x1, starting transfers between devices, body(): lax.all_to_all(jnp.stack([layer_keeps[None]] * lax.axis_size('depth')), '...  13.1 us
  transfers between devices with their start and end apart: 17, of which 17 were waited for; matrix products, arithmetic and copies ran while one was open for 5% of the time, Pallas kernels for 0%

profile of v1, /device:TPU:1, one launch (start us, length us, event | category | flops | bytes accessed | tf_op | source)
XLA Modules:
  0.0 449.2 jit_solution(6436275001941145879)
XLA Ops:
  6.5 1.4 scatter_custom_fusion
  8.6 10.5 %all-to-all-start = ((s32[32,1,8]{2,1,0:T(1,128)}), s32[32,1,8]{2,1,0:T(1,128)S(1)}, u32[]{:S(2)}, u32[]{:S(2)}) async-start(s32[32,1,8]{2,1,0:T(1,128)} %bitcast.92), calls=%async_computation | async-start | bytes 32768 | tf_op jit(solution)/shard_map/all_to_all | solution.py:187
  19.9 1.2 scatter_custom_fusion.3
  21.9 1.2 scatter_custom_fusion.1
  23.1 2.9 all-to-all-done
  26.1 4.6 %all-to-all-start.2 = ((f32[32,8,6]{2,1,0:T(8,128)}), f32[32,8,6]{2,1,0:T(8,128)S(1)}, u32[]{:S(2)}, u32[]{:S(2)}) async-start(f32[32,8,6]{2,1,0:T(8,128)} %slice_bitcast_fusion.15), calls=%async_computation.2 | async-start | bytes 262144 | tf_op jit(solution)/shard_map/all_to_all | solution.py:189
  32.6 5.7 %all-to-all-done.2 = f32[32,8,6]{2,1,0:T(8,128)S(1)} async-done(((f32[32,8,6]{2,1,0:T(8,128)}), f32[32,8,6]{2,1,0:T(8,128)S(1)}, u32[]{:S(2)}, u32[]{:S(2)}) %all-to-all-start.2) | async-done | bytes 6176 | tf_op jit(solution)/shard_map/all_to_all | solution.py:189
  38.2 3.9 all-to-all-start.1
  42.2 1.2 scatter_custom_fusion.4
  43.4 6.2 %all-to-all-done.1 = bf16[32,8,128]{2,1,0:T(8,128)(2,1)S(1)} async-done(((bf16[32,8,128]{2,1,0:T(8,128)(2,1)}), bf16[32,8,128]{2,1,0:T(8,128)(2,1)S(1)}, u32[]{:S(2)}, u32[]{:S(2)}) %all-to-all-start.1) | async-done | bytes 65568 | tf_op jit(solution)/shard_map/all_to_all | solution.py:186
  49.6 1.2 scatter_custom_fusion.2
  52.3 5.0 %while.88 = (s32[]{:T(128)}, f32[2,128,1024]{1,2,0:T(8,128)S(1)}, f32[2,1024]{1,0:T(2,128)S(1)}, bf16[2,128,128]{2,1,0:T(8,128)(2,1)S(1)}, f32[2,6,128]{2,1,0:T(8,128)S(1)}, /*index=5*/s32[]{:T(128)}, s32[]{:T(128)}) while((s32[]{:T(128)}, f32[2,128,1024]{1,2,0:T(8,128)S(1)}, f32[2,1024]{1,0:T(2,128)S(1)}, ...), condition=%wide.region_11.12_spmd, body=%wide.region_8.11_spmd.sunk | while | flops 242777600 | bytes 1177685 | solution.py:206
  52.8 1.2 fusion.322
  55.3 1.2 fusion.322
  57.9 13.1 %all-to-all-start.3 = ((f32[16,1,2,1024]{3,2,1,0:T(2,128)}), f32[16,1,2,1024]{3,2,1,0:T(2,128)S(1)}, u32[]{:S(2)}, u32[]{:S(2)}) async-start(f32[16,1,2,1024]{3,2,1,0:T(2,128)} %stack.44), calls=%async_computation.3 | async-start | bytes 262144 | tf_op jit(solution)/shard_map/all_to_all | solution.py:208
  71.0 12.1 %all-to-all-done.3 = f32[16,1,2,1024]{3,2,1,0:T(2,128)S(1)} async-done(((f32[16,1,2,1024]{3,2,1,0:T(2,128)}), f32[16,1,2,1024]{3,2,1,0:T(2,128)S(1)}, u32[]{:S(2)}, u32[]{:S(2)}) %all-to-all-start.3) | async-done | bytes 131104 | tf_op jit(solution)/shard_map/all_to_all | solution.py:208
  83.6 0.8 copy.118
  84.4 6.5 %all-to-all-start.4 = ((bf16[16,2,128,64]{2,3,1,0:T(8,128)(2,1)}), bf16[16,2,128,64]{2,3,1,0:T(8,128)(2,1)S(1)}, u32[]{:S(2)}, u32[]{:S(2)}) async-start(bf16[16,2,128,64]{2,3,1,0:T(8,128)(2,1)} %copy.118), calls=%async_computation.4 | async-start | bytes 1048576 | tf_op jit(solution)/shard_map/all_to_all | solution.py:25
  91.2 22.7 %all-to-all-done.4 = bf16[16,2,128,64]{2,3,1,0:T(8,128)(2,1)S(1)} async-done(((bf16[16,2,128,64]{2,3,1,0:T(8,128)(2,1)}), bf16[16,2,128,64]{2,3,1,0:T(8,128)(2,1)S(1)}, u32[]{:S(2)}, u32[]{:S(2)}) %all-to-all-start.4) | async-done | bytes 524320 | tf_op jit(solution)/shard_map/all_to_all | solution.py:25
  114.0 1.1 broadcast_in_dim.225
  115.1 12.5 %all-to-all-start.6 = ((f32[16,2,128,64]{2,3,1,0:T(8,128)}), f32[16,2,128,64]{2,3,1,0:T(8,128)S(1)}, u32[]{:S(2)}, u32[]{:S(2)}) async-start(f32[16,2,128,64]{2,3,1,0:T(8,128)} %broadcast_in_dim.225), calls=%async_computation.6 | async-start | bytes 2097152 | tf_op jit(solution)/shard_map/all_to_all | solution.py:37
  127.6 1.4 scatter_custom_fusion.5
  129.7 43.0 %all-to-all-done.6 = f32[16,2,128,64]{2,3,1,0:T(8,128)S(1)} async-done(((f32[16,2,128,64]{2,3,1,0:T(8,128)}), f32[16,2,128,64]{2,3,1,0:T(8,128)S(1)}, u32[]{:S(2)}, u32[]{:S(2)}) %all-to-all-start.6) | async-done | bytes 1048608 | tf_op jit(solution)/shard_map/all_to_all | solution.py:37
  172.8 9.2 %all-to-all-start.5 = ((s32[32,1,8]{2,1,0:T(1,128)}), s32[32,1,8]{2,1,0:T(1,128)S(1)}, u32[]{:S(2)}, u32[]{:S(2)}) async-start(s32[32,1,8]{2,1,0:T(1,128)} %bitcast.113), calls=%async_computation.5 | async-start | bytes 32768 | tf_op jit(solution)/shard_map/all_to_all | solution.py:187
  182.8 6.2 %all-to-all-done.5 = s32[32,1,8]{2,1,0:T(1,128)S(1)} async-done(((s32[32,1,8]{2,1,0:T(1,128)}), s32[32,1,8]{2,1,0:T(1,128)S(1)}, u32[]{:S(2)}, u32[]{:S(2)}) %all-to-all-start.5) | async-done | bytes 1056 | tf_op jit(solution)/shard_map/all_to_all | solution.py:187
  189.7 7.6 %all-to-all-start.7 = ((f32[16,1,2,1024]{3,2,1,0:T(2,128)}), f32[16,1,2,1024]{3,2,1,0:T(2,128)S(1)}, u32[]{:S(2)}, u32[]{:S(2)}) async-start(f32[16,1,2,1024]{3,2,1,0:T(2,128)} %broadcast_in_dim.226), calls=%async_computation.7 | async-start | bytes 262144 | tf_op jit(solution)/shard_map/all_to_all | solution.py:37
  198.3 11.0 %all-to-all-done.7 = f32[16,1,2,1024]{3,2,1,0:T(2,128)S(1)} async-done(((f32[16,1,2,1024]{3,2,1,0:T(2,128)}), f32[16,1,2,1024]{3,2,1,0:T(2,128)S(1)}, u32[]{:S(2)}, u32[]{:S(2)}) %all-to-all-start.7) | async-done | bytes 131104 | tf_op jit(solution)/shard_map/all_to_all | solution.py:37
  209.3 0.8 while.92
  210.2 9.2 %while.89 = (s32[]{:T(128)}, f32[2,128,128]{2,1,0:T(8,128)S(1)}, f32[2,6,128]{2,1,0:T(8,128)S(1)}, f32[2,6,128]{2,1,0:T(8,128)S(1)}, bf16[2,128,1024]{1,2,0:T(8,...) while((s32[]{:T(128)}, f32[2,128,128]{2,1,0:T(8,128)S(1)}, ...), condition=%wide.region_31.32_spmd, body=%wide.region_21.31_spmd.sunk | while | flops 485672448 | bytes 3947105 | solution.py:230
  212.2 1.9 fusion.332
  216.8 1.9 fusion.332
  220.3 0.8 bitcast_select_fusion.2
  221.0 7.2 %all-to-all-start.10 = ((f32[32,8,6]{2,1,0:T(8,128)}), f32[32,8,6]{2,1,0:T(8,128)S(1)}, u32[]{:S(2)}, u32[]{:S(2)}) async-start(f32[32,8,6]{2,1,0:T(8,128)} %bitcast_select_fusion.2), calls=%async_computation.10 | async-start | bytes 262144 | tf_op jit(solution)/shard_map/all_to_all | solution.py:244
  229.8 6.2 %all-to-all-done.10 = f32[32,8,6]{2,1,0:T(8,128)S(1)} async-done(((f32[32,8,6]{2,1,0:T(8,128)}), f32[32,8,6]{2,1,0:T(8,128)S(1)}, u32[]{:S(2)}, u32[]{:S(2)}) %all-to-all-start.10) | async-done | bytes 6176 | tf_op jit(solution)/shard_map/all_to_all | solution.py:244
  236.0 3.9 all-to-all-start.8
  241.0 1.2 scatter_custom_fusion.8
  242.9 4.8 %all-to-all-done.8 = f32[32,8,128]{2,1,0:T(8,128)S(1)} async-done(((f32[32,8,128]{2,1,0:T(8,128)}), f32[32,8,128]{2,1,0:T(8,128)S(1)}, u32[]{:S(2)}, u32[]{:S(2)}) %all-to-all-start.8) | async-done | bytes 131104 | tf_op jit(solution)/shard_map/all_to_all | solution.py:243
  247.6 3.9 all-to-all-start.11
  252.3 1.2 scatter_custom_fusion.6
  254.1 5.1 %all-to-all-done.11 = f32[32,8,6]{2,1,0:T(8,128)S(1)} async-done(((f32[32,8,6]{2,1,0:T(8,128)}), f32[32,8,6]{2,1,0:T(8,128)S(1)}, u32[]{:S(2)}, u32[]{:S(2)}) %all-to-all-start.11) | async-done | bytes 6176 | tf_op jit(solution)/shard_map/all_to_all | solution.py:189
  259.3 3.9 all-to-all-start.9
  263.2 1.2 scatter_custom_fusion.9
  264.5 6.2 %all-to-all-done.9 = bf16[32,8,128]{2,1,0:T(8,128)(2,1)S(1)} async-done(((bf16[32,8,128]{2,1,0:T(8,128)(2,1)}), bf16[32,8,128]{2,1,0:T(8,128)(2,1)S(1)}, u32[]{:S(2)}, u32[]{:S(2)}) %all-to-all-start.9) | async-done | bytes 65568 | tf_op jit(solution)/shard_map/all_to_all | solution.py:186
  270.6 1.4 scatter_custom_fusion.7
  273.5 5.0 %while.90 = (s32[]{:T(128)}, f32[2,128,1024]{1,2,0:T(8,128)S(1)}, f32[2,1024]{1,0:T(2,128)S(1)}, bf16[2,128,128]{2,1,0:T(8,128)(2,1)S(1)}, f32[2,6,128]{2,1,0:T(8,128)S(1)}, /*index=5*/s32[]{:T(128)}, s32[]{:T(128)}) while((s32[]{:T(128)}, f32[2,128,1024]{1,2,0:T(8,128)S(1)}, f32[2,1024]{1,0:T(2,128)S(1)}, ...), condition=%wide.region_39.40_spmd, body=%wide.region_36.39_spmd.sunk | while | flops 242777600 | bytes 1177685 | solution.py:206
  274.0 1.2 fusion.338
  276.5 1.2 fusion.338
  278.5 15.4 %all_to_all.98 = f32[16,1,2,1024]{3,2,1,0:T(2,128)S(1)} all-to-all(f32[16,1,2,1024]{3,2,1,0:T(2,128)S(1)} %stack.45), channel_id=1, replica_groups=mesh['tile'=32,'depth'=16] {'depth'}, dimensions={0} | all-to-all | bytes 262144 | tf_op jit(solution)/shard_map/all_to_all | solution.py:208
  294.4 0.8 copy.132
  295.2 6.5 %all-to-all-start.13 = ((bf16[16,2,128,64]{2,3,1,0:T(8,128)(2,1)}), bf16[16,2,128,64]{2,3,1,0:T(8,128)(2,1)S(1)}, u32[]{:S(2)}, u32[]{:S(2)}) async-start(bf16[16,2,128,64]{2,3,1,0:T(8,128)(2,1)} %copy.132), calls=%async_computation.13 | async-start | bytes 1048576 | tf_op jit(solution)/shard_map/all_to_all | solution.py:25
  302.0 22.8 %all-to-all-done.13 = bf16[16,2,128,64]{2,3,1,0:T(8,128)(2,1)S(1)} async-done(((bf16[16,2,128,64]{2,3,1,0:T(8,128)(2,1)}), bf16[16,2,128,64]{2,3,1,0:T(8,128)(2,1)S(1)}, u32[]{:S(2)}, u32[]{:S(2)}) %all-to-all-start.13) | async-done | bytes 524320 | tf_op jit(solution)/shard_map/all_to_all | solution.py:25
  324.8 1.1 broadcast_in_dim.231
  325.9 12.5 %all-to-all-start.14 = ((f32[16,2,128,64]{2,3,1,0:T(8,128)}), f32[16,2,128,64]{2,3,1,0:T(8,128)S(1)}, u32[]{:S(2)}, u32[]{:S(2)}) async-start(f32[16,2,128,64]{2,3,1,0:T(8,128)} %broadcast_in_dim.231), calls=%async_computation.14 | async-start | bytes 2097152 | tf_op jit(solution)/shard_map/all_to_all | solution.py:37
  338.5 45.1 %all-to-all-done.14 = f32[16,2,128,64]{2,3,1,0:T(8,128)S(1)} async-done(((f32[16,2,128,64]{2,3,1,0:T(8,128)}), f32[16,2,128,64]{2,3,1,0:T(8,128)S(1)}, u32[]{:S(2)}, u32[]{:S(2)}) %all-to-all-start.14) | async-done | bytes 1048608 | tf_op jit(solution)/shard_map/all_to_all | solution.py:37
  385.1 12.9 %all-to-all-start.15 = ((f32[16,1,2,1024]{3,2,1,0:T(2,128)}), f32[16,1,2,1024]{3,2,1,0:T(2,128)S(1)}, u32[]{:S(2)}, u32[]{:S(2)}) async-start(f32[16,1,2,1024]{3,2,1,0:T(2,128)} %broadcast_in_dim.232), calls=%async_computation.15 | async-start | bytes 262144 | tf_op jit(solution)/shard_map/all_to_all | solution.py:37
  398.8 11.1 %all-to-all-done.15 = f32[16,1,2,1024]{3,2,1,0:T(2,128)S(1)} async-done(((f32[16,1,2,1024]{3,2,1,0:T(2,128)}), f32[16,1,2,1024]{3,2,1,0:T(2,128)S(1)}, u32[]{:S(2)}, u32[]{:S(2)}) %all-to-all-start.15) | async-done | bytes 131104 | tf_op jit(solution)/shard_map/all_to_all | solution.py:37
  409.9 0.8 while.93
  410.8 9.1 %while.91 = (s32[]{:T(128)}, f32[2,128,128]{2,1,0:T(8,128)S(1)}, f32[2,6,128]{2,1,0:T(8,128)S(1)}, f32[2,6,128]{2,1,0:T(8,128)S(1)}, bf16[2,128,1024]{1,2,0:T(8,...) while((s32[]{:T(128)}, f32[2,128,128]{2,1,0:T(8,128)S(1)}, ...), condition=%wide.region_55.56_spmd, body=%wide.region_45.55_spmd.sunk | while | flops 485672448 | bytes 3947105 | solution.py:230
  412.8 1.9 fusion.348
  417.4 1.9 fusion.348
  421.6 6.9 %all-to-all-start.17 = ((f32[32,8,6]{2,1,0:T(8,128)}), f32[32,8,6]{2,1,0:T(8,128)S(1)}, u32[]{:S(2)}, u32[]{:S(2)}) async-start(f32[32,8,6]{2,1,0:T(8,128)} %bitcast_select_fusion), calls=%async_computation.17 | async-start | bytes 262144 | tf_op jit(solution)/shard_map/all_to_all | solution.py:244
  429.9 6.2 %all-to-all-done.17 = f32[32,8,6]{2,1,0:T(8,128)S(1)} async-done(((f32[32,8,6]{2,1,0:T(8,128)}), f32[32,8,6]{2,1,0:T(8,128)S(1)}, u32[]{:S(2)}, u32[]{:S(2)}) %all-to-all-start.17) | async-done | bytes 6176 | tf_op jit(solution)/shard_map/all_to_all | solution.py:244
  436.2 3.9 all-to-all-start.16
  442.3 5.5 %all-to-all-done.16 = f32[32,8,128]{2,1,0:T(8,128)S(1)} async-done(((f32[32,8,128]{2,1,0:T(8,128)}), f32[32,8,128]{2,1,0:T(8,128)S(1)}, u32[]{:S(2)}, u32[]{:S(2)}) %all-to-all-start.16) | async-done | bytes 131104 | tf_op jit(solution)/shard_map/all_to_all | solution.py:243
  (277 shorter events, 48.9 us)
Async XLA Ops:
  2.2 0.6 copy-start.6
  3.6 0.6 copy-start.7
  4.2 0.7 slice-start.2
  5.0 0.7 slice-start.3
  5.8 0.7 copy-start.5
  8.6 10.5 %copy-start.4 = (f32[2,1,5,256]{3,1,2,0:T(1,128)S(1)}, f32[2,1,5,256]{3,1,2,0:T(1,128)}, u32[]{:S(2)}) copy-start(f32[2,1,5,256]{3,1,2,0:T(1,128)} %param.19) | copy-start | bytes 30724
  8.6 17.5 %all-to-all-start = ((s32[32,1,8]{2,1,0:T(1,128)}), s32[32,1,8]{2,1,0:T(1,128)S(1)}, u32[]{:S(2)}, u32[]{:S(2)}) async-start(s32[32,1,8]{2,1,0:T(1,128)} %bitcast.92), calls=%async_computation | async-start | bytes 32768 | tf_op jit(solution)/shard_map/all_to_all | solution.py:187
  19.1 0.7 copy-start.8
  21.1 0.8 copy-start.3
  26.1 12.2 %all-to-all-start.2 = ((f32[32,8,6]{2,1,0:T(8,128)}), f32[32,8,6]{2,1,0:T(8,128)S(1)}, u32[]{:S(2)}, u32[]{:S(2)}) async-start(f32[32,8,6]{2,1,0:T(8,128)} %slice_bitcast_fusion.15), calls=%async_computation.2 | async-start | bytes 262144 | tf_op jit(solution)/shard_map/all_to_all | solution.py:189
  38.2 11.4 %all-to-all-start.1 = ((bf16[32,8,128]{2,1,0:T(8,128)(2,1)}), bf16[32,8,128]{2,1,0:T(8,128)(2,1)S(1)}, u32[]{:S(2)}, u32[]{:S(2)}) async-start(bf16[32,8,128]{2,1,0:T(8,128)(2,1)} %slice_bitcast_fusion.17), calls=%async_computation.1 | async-start | bytes 131072 | tf_op jit(solution)/shard_map/all_to_all | solution.py:186
  50.8 0.6 copy-start.1
  51.4 0.8 slice-start
  57.9 25.2 %all-to-all-start.3 = ((f32[16,1,2,1024]{3,2,1,0:T(2,128)}), f32[16,1,2,1024]{3,2,1,0:T(2,128)S(1)}, u32[]{:S(2)}, u32[]{:S(2)}) async-start(f32[16,1,2,1024]{3,2,1,0:T(2,128)} %stack.44), calls=%async_computation.3 | async-start | bytes 262144 | tf_op jit(solution)/shard_map/all_to_all | solution.py:208
  83.6 7.4 %copy-start = (bf16[2,2,128,1024]{3,2,1,0:T(8,128)(2,1)S(1)}, bf16[2,2,128,1024]{3,2,1,0:T(8,128)(2,1)}, u32[]{:S(2)}) copy-start(bf16[2,2,128,1024]{3,2,1,0:T(8,128)(2,1)} %param.21) | copy-start | bytes 3145732
  84.4 29.5 %all-to-all-start.4 = ((bf16[16,2,128,64]{2,3,1,0:T(8,128)(2,1)}), bf16[16,2,128,64]{2,3,1,0:T(8,128)(2,1)S(1)}, u32[]{:S(2)}, u32[]{:S(2)}) async-start(bf16[16,2,128,64]{2,3,1,0:T(8,128)(2,1)} %copy.118), calls=%async_computation.4 | async-start | bytes 1048576 | tf_op jit(solution)/shard_map/all_to_all | solution.py:25
  115.1 57.7 %all-to-all-start.6 = ((f32[16,2,128,64]{2,3,1,0:T(8,128)}), f32[16,2,128,64]{2,3,1,0:T(8,128)S(1)}, u32[]{:S(2)}, u32[]{:S(2)}) async-start(f32[16,2,128,64]{2,3,1,0:T(8,128)} %broadcast_in_dim.225), calls=%async_computation.6 | async-start | bytes 2097152 | tf_op jit(solution)/shard_map/all_to_all | solution.py:37
  172.8 16.2 %all-to-all-start.5 = ((s32[32,1,8]{2,1,0:T(1,128)}), s32[32,1,8]{2,1,0:T(1,128)S(1)}, u32[]{:S(2)}, u32[]{:S(2)}) async-start(s32[32,1,8]{2,1,0:T(1,128)} %bitcast.113), calls=%async_computation.5 | async-start | bytes 32768 | tf_op jit(solution)/shard_map/all_to_all | solution.py:187
  189.7 19.6 %all-to-all-start.7 = ((f32[16,1,2,1024]{3,2,1,0:T(2,128)}), f32[16,1,2,1024]{3,2,1,0:T(2,128)S(1)}, u32[]{:S(2)}, u32[]{:S(2)}) async-start(f32[16,1,2,1024]{3,2,1,0:T(2,128)} %broadcast_in_dim.226), calls=%async_computation.7 | async-start | bytes 262144 | tf_op jit(solution)/shard_map/all_to_all | solution.py:37
  221.0 15.0 %all-to-all-start.10 = ((f32[32,8,6]{2,1,0:T(8,128)}), f32[32,8,6]{2,1,0:T(8,128)S(1)}, u32[]{:S(2)}, u32[]{:S(2)}) async-start(f32[32,8,6]{2,1,0:T(8,128)} %bitcast_select_fusion.2), calls=%async_computation.10 | async-start | bytes 262144 | tf_op jit(solution)/shard_map/all_to_all | solution.py:244
  236.0 11.6 %all-to-all-start.8 = ((f32[32,8,128]{2,1,0:T(8,128)}), f32[32,8,128]{2,1,0:T(8,128)S(1)}, u32[]{:S(2)}, u32[]{:S(2)}) async-start(f32[32,8,128]{2,1,0:T(8,128)} %bitcast_select_fusion.3), calls=%async_computation.8 | async-start | bytes 262144 | tf_op jit(solution)/shard_map/all_to_all | solution.py:243
  247.6 11.6 %all-to-all-start.11 = ((f32[32,8,6]{2,1,0:T(8,128)}), f32[32,8,6]{2,1,0:T(8,128)S(1)}, u32[]{:S(2)}, u32[]{:S(2)}) async-start(f32[32,8,6]{2,1,0:T(8,128)} %slice_bitcast_fusion.14), calls=%async_computation.11 | async-start | bytes 262144 | tf_op jit(solution)/shard_map/all_to_all | solution.py:189
  259.3 11.4 %all-to-all-start.9 = ((bf16[32,8,128]{2,1,0:T(8,128)(2,1)}), bf16[32,8,128]{2,1,0:T(8,128)(2,1)S(1)}, u32[]{:S(2)}, u32[]{:S(2)}) async-start(bf16[32,8,128]{2,1,0:T(8,128)(2,1)} %slice_bitcast_fusion.16), calls=%async_computation.9 | async-start | bytes 131072 | tf_op jit(solution)/shard_map/all_to_all | solution.py:186
  272.0 0.6 copy-start.2
  272.6 0.8 slice-start.1
  295.2 29.5 %all-to-all-start.13 = ((bf16[16,2,128,64]{2,3,1,0:T(8,128)(2,1)}), bf16[16,2,128,64]{2,3,1,0:T(8,128)(2,1)S(1)}, u32[]{:S(2)}, u32[]{:S(2)}) async-start(bf16[16,2,128,64]{2,3,1,0:T(8,128)(2,1)} %copy.132), calls=%async_computation.13 | async-start | bytes 1048576 | tf_op jit(solution)/shard_map/all_to_all | solution.py:25
  325.9 57.7 %all-to-all-start.14 = ((f32[16,2,128,64]{2,3,1,0:T(8,128)}), f32[16,2,128,64]{2,3,1,0:T(8,128)S(1)}, u32[]{:S(2)}, u32[]{:S(2)}) async-start(f32[16,2,128,64]{2,3,1,0:T(8,128)} %broadcast_in_dim.231), calls=%async_computation.14 | async-start | bytes 2097152 | tf_op jit(solution)/shard_map/all_to_all | solution.py:37
  385.1 24.9 %all-to-all-start.15 = ((f32[16,1,2,1024]{3,2,1,0:T(2,128)}), f32[16,1,2,1024]{3,2,1,0:T(2,128)S(1)}, u32[]{:S(2)}, u32[]{:S(2)}) async-start(f32[16,1,2,1024]{3,2,1,0:T(2,128)} %broadcast_in_dim.232), calls=%async_computation.15 | async-start | bytes 262144 | tf_op jit(solution)/shard_map/all_to_all | solution.py:37
  421.6 14.6 %all-to-all-start.17 = ((f32[32,8,6]{2,1,0:T(8,128)}), f32[32,8,6]{2,1,0:T(8,128)S(1)}, u32[]{:S(2)}, u32[]{:S(2)}) async-start(f32[32,8,6]{2,1,0:T(8,128)} %bitcast_select_fusion), calls=%async_computation.17 | async-start | bytes 262144 | tf_op jit(solution)/shard_map/all_to_all | solution.py:244
  436.2 11.6 %all-to-all-start.16 = ((f32[32,8,128]{2,1,0:T(8,128)}), f32[32,8,128]{2,1,0:T(8,128)S(1)}, u32[]{:S(2)}, u32[]{:S(2)}) async-start(f32[32,8,128]{2,1,0:T(8,128)} %bitcast_select_fusion.1), calls=%async_computation.16 | async-start | bytes 262144 | tf_op jit(solution)/shard_map/all_to_all | solution.py:243
